TPU v7x, 512 devices: a whole 4x4x16 slice. The times are simulated.
512 devices in a mesh: req: 128 (over z, x, core), tp: 4 (over y).
Axes of the slice: x: 4, y: 4, z: 16, core: 2. Of those that a mesh axis runs over, the one named last changes fastest.
Arguments:
- tokens: bfloat16 [65536, 1408], P('req', 'tp'), may hold values from -24 to 24
- ln1_gain: float32 [1408], replicated, may hold values from 0.1 to 1.9
- ln1_bias: float32 [1408], replicated, may hold values from -3 to 3
- qkv_weight: bfloat16 [3, 1408, 1408], P(None, None, 'tp'), may hold values from -6 to 6
- out_weight: bfloat16 [1408, 1408], P('tp'), may hold values from -0.15625 to 0.15625
- ln2_gain: float32 [1408], replicated, may hold values from 0.25 to 1.75
- ln2_bias: float32 [1408], replicated, may hold values from -3 to 3
- merger_weight: bfloat16 [5632, 3584], P('req', 'tp'), may hold values from -0.078125 to 0.078125
- group_segments: int32 [128, 128], P('req'), may hold values from 0 to 7, never falling along the last dimension, each value on 1 to 41 neighbouring positions
- owners: int32 [16384, 1], P('req'), may hold values from 0 to 127; in each aligned block of 128 rows (0 to 127, 128 to 255, ...) at most 2 rows name the same one
Outputs:
- received: bfloat16 [32768, 3584], P('req', 'tp')
Inputs may be any that keep to these rules, and one draw needn't show every extreme that they name: `group_segments`: never falling along a request's groups; every picture has 1 to 41 groups and one has exactly 41. `owners`: among the 128 groups of one request no owner appears more than 2 times; in every draw some request sends exactly 2 to some owner.
All inputs are finite; a program needn't handle non-finite values.
Results may differ from a plain program's by a relative error of at most 0.009.
Values may be sent and summed in bfloat16 or wider, within the bound.
No kernel may reach another device: no remote copies, remote signals or barrier semaphores. Data moves between devices by JAX's collectives and lax.ppermute only.
A program may use at most 128 MiB of HBM per device.

v0:
```python
import jax
import jax.numpy as jnp
from jax import lax
from jax.sharding import PartitionSpec as P

HEAD_DIM = 88
epsilon = 1e-06


def local(
    tokens,
    ln1_gain,
    ln1_bias,
    qkv_weight,
    out_weight,
    ln2_gain,
    ln2_bias,
    merger_weight,
    group_segments,
    owners,
):
    tp_count = lax.axis_size("tp")
    req_count = lax.axis_size("req")
    col_width = tokens.shape[1]
    full_width = col_width * tp_count
    tok_count = tokens.shape[0]
    group_count = tok_count // 4
    out_cols = merger_weight.shape[1]
    gathered = lax.all_gather(tokens, "tp", axis=1, tiled=True).astype(jnp.float32)
    input_mean = jnp.mean(gathered, axis=1, keepdims=True)
    centered = gathered - input_mean
    input_var = jnp.mean(centered * centered, axis=1, keepdims=True)
    normed = (centered * lax.rsqrt(input_var + epsilon) * ln1_gain + ln1_bias).astype(jnp.bfloat16)
    combined = jnp.einsum("td,cdh->cth", normed, qkv_weight, preferred_element_type=jnp.float32)
    combined = combined.astype(jnp.bfloat16).reshape(3, tok_count, -1, HEAD_DIM)
    queries, key_heads, value_heads = (combined[0], combined[1], combined[2])
    segment_ids = jnp.repeat(group_segments[0], 4)
    same_picture = segment_ids[:, None] == segment_ids[None, :]
    scores = jnp.einsum(
        "qhd,khd->hqk", queries, key_heads, preferred_element_type=jnp.float32
    ) * HEAD_DIM ** (-0.5)
    scores = jnp.where(same_picture[None], scores, -1e30)
    row_max = jnp.max(scores, axis=2, keepdims=True)
    exponent = jnp.exp(scores - row_max)
    weights = (exponent / jnp.sum(exponent, axis=2, keepdims=True)).astype(jnp.bfloat16)
    context = jnp.einsum("hqk,khd->qhd", weights, value_heads, preferred_element_type=jnp.float32)
    context = context.astype(jnp.bfloat16).reshape(tok_count, -1)
    partial_value = jnp.dot(context, out_weight, preferred_element_type=jnp.float32)
    attended = lax.psum_scatter(
        partial_value.astype(jnp.bfloat16), "tp", scatter_dimension=1, tiled=True
    ).astype(jnp.float32)
    hidden = tokens.astype(jnp.float32) + attended
    row_total = lax.psum(jnp.sum(hidden, axis=1), "tp")
    row_mean = (row_total / full_width)[:, None]
    shifted = hidden - row_mean
    row_spread = lax.psum(jnp.sum(shifted * shifted, axis=1), "tp")
    variance = (row_spread / full_width)[:, None]
    offset = lax.axis_index("tp") * col_width
    gain_part = lax.dynamic_slice_in_dim(ln2_gain, offset, col_width)
    bias_part = lax.dynamic_slice_in_dim(ln2_bias, offset, col_width)
    patches = (shifted * lax.rsqrt(variance + epsilon) * gain_part + bias_part).astype(jnp.bfloat16)
    grouped = patches.reshape(group_count, 4, col_width)
    full_groups = lax.all_gather(grouped, "tp", axis=2, tiled=True)
    merged = full_groups.reshape(group_count, 4 * full_width)
    projected = jnp.dot(
        merged,
        lax.all_gather(merger_weight, "req", axis=0, tiled=True),
        preferred_element_type=jnp.float32,
    )
    projected = projected.astype(jnp.bfloat16)
    capacity = max(2, 2 * group_count // req_count)
    slot_count = req_count * capacity
    target = owners[:, 0]
    owner_ids = jnp.arange(req_count, dtype=jnp.int32)
    owner_hits = (target[:, None] == owner_ids[None, :]).astype(jnp.int32)
    before = jnp.cumsum(owner_hits, axis=0) - owner_hits
    slot_rank = jnp.sum(before * owner_hits, axis=1)
    slot_index = target * capacity + slot_rank
    placing = (slot_index[None, :] == jnp.arange(slot_count, dtype=jnp.int32)[:, None]).astype(
        jnp.bfloat16
    )
    outgoing = jnp.dot(placing, projected, preferred_element_type=jnp.float32).astype(jnp.bfloat16)
    outgoing = outgoing.reshape(req_count, capacity, out_cols)
    arrived = lax.all_to_all(outgoing, "req", split_axis=0, concat_axis=0, tiled=True)
    return arrived.reshape(slot_count, out_cols)


def solution(mesh):
    in_specs = (
        P("req", "tp"),
        P(),
        P(),
        P(None, None, "tp"),
        P("tp", None),
        P(),
        P(),
        P("req", "tp"),
        P("req", None),
        P("req", None),
    )
    out_specs = P("req", "tp")
    return jax.shard_map(local, mesh=mesh, in_specs=in_specs, out_specs=out_specs, check_vma=False)
```

profile of v0, /device:TPU:33, one launch (start us, length us, event | category | flops | bytes accessed | tf_op | source)
XLA Modules:
  0.0 379.6 jit_solution(7323851090388105527)
XLA Ops:
  8.3 0.9 broadcast_compare_fusion
  9.3 37.2 %all-gather.5.cloned.1.call-done = bf16[512,1408]{0,1:T(8,128)(2,1)} async-done(((bf16[512,352]{0,1:T(8,128)(2,1)}), bf16[512,1408]{0,1:T(8,128)(2,1)}) %all-gather.5.cloned.1.call-update) | async-done | bytes 1441808 | tf_op jit(solution)/shard_map/all_gather | solution.py:29
  46.5 1.7 convert_reduce_fusion
  48.2 1.8 fusion.4
  50.1 2.0 fusion.18
  53.0 4.8 %fusion.31 = (f32[4,512]{1,0:T(4,128)S(1)}, f32[4,512,512]{1,2,0:T(8,128)}) fusion(pred[512,512]{0,1:T(8,128)(4,1)} %broadcast_compare_fusion, bf16[512,4,88]{0,2,1:T(8,128)(2,1)} %bitcast.31, bf16[512,4,88]{0,2,1:T(8,128)(2,1)} %bitcast.30), kind=kOutput, calls=%fused_computation.48 | convolution fusion | flops 188744192 | bytes 5185536 | tf_op jit(solution)/shard_map/sub | solution.py:44
  57.8 2.8 fusion.21
  60.6 2.1 convolution_convert_fusion
  64.3 30.7 %reduce-scatter.2.cloned.1.call-done = bf16[512,352]{0,1:T(8,128)(2,1)} async-done(((bf16[512,1408]{0,1:T(8,128)(2,1)}), bf16[512,352]{0,1:T(8,128)(2,1)}) %reduce-scatter.2.cloned.1.call-update) | async-done | bytes 360464 | tf_op jit(solution)/shard_map/reduce_scatter | solution.py:49
  95.0 1.1 fusion.23
  96.1 7.6 %psum.14 = f32[512]{0:T(512)S(1)} all-reduce(f32[512]{0:T(512)S(1)} %fusion.23), channel_id=1, replica_groups=mesh['req'=128,'tp'=4] {'tp'}, use_global_device_ids=true, to_apply=%region_8.9 | all-reduce | flops 512 | bytes 4096 | tf_op jit(solution)/shard_map/psum | solution.py:53
  103.7 1.1 multiply_reduce_fusion
  104.9 6.0 %psum.15 = f32[512]{0:T(512)S(1)} all-reduce(f32[512]{0:T(512)S(1)} %multiply_reduce_fusion), channel_id=1, replica_groups=mesh['req'=128,'tp'=4] {'tp'}, use_global_device_ids=true, to_apply=%region_10.11 | all-reduce | flops 512 | bytes 4096 | tf_op jit(solution)/shard_map/psum | solution.py:56
  110.9 1.9 add_convert_fusion
  112.8 1.2 copy.19
  114.8 2.1 copy.20
  118.0 36.7 %all-gather.7.cloned.1.call-done = bf16[128,4,1408]{0,1,2:T(4,128)(2,1)} async-done(((bf16[128,4,352]{0,1,2:T(4,128)(2,1)}), bf16[128,4,1408]{0,1,2:T(4,128)(2,1)}) %all-gather.7.cloned.1.call-update) | async-done | bytes 1441808 | tf_op jit(solution)/shard_map/all_gather | solution.py:63
  154.7 2.7 copy.21
  157.4 151.2 %all-gather.9.cloned.1.call-done = bf16[128,44,896]{2,1,0:T(8,128)(2,1)} async-done(((bf16[1,44,896]{2,1,0:T(8,128)(2,1)}), bf16[128,44,896]{2,1,0:T(8,128)(2,1)}) %all-gather.9.cloned.1.call-update) | async-done | bytes 10092560 | tf_op jit(solution)/shard_map/all_gather | solution.py:67
  308.6 13.4 %reshape.91 = bf16[5632,896]{1,0:T(8,128)(2,1)} reshape(bf16[128,44,896]{2,1,0:T(8,128)(2,1)} %all-gather.9.cloned.1.call-done) | data formatting | bytes 20185088
  322.0 7.0 %convolution_convert_fusion.2 = bf16[256,896]{1,0:T(8,128)(2,1)} fusion(bf16[128,5632]{0,1:T(8,128)(2,1)} %bitcast.28, bf16[5632,896]{1,0:T(8,128)(2,1)} %reshape.91, s32[128]{0:T(128)S(1)} %multiply_add_fusion), kind=kOutput, calls=%fused_computation.25 | convolution fusion | flops 1350942720 | bytes 11993600 | tf_op jit(solution)/shard_map/dot_general | solution.py:82
  329.0 1.2 reshape.88
  330.2 40.9 %all_to_all.5 = bf16[128,2,896]{2,1,0:T(2,128)(2,1)} all-to-all(bf16[128,2,896]{2,1,0:T(2,128)(2,1)S(1)} %reshape.88), channel_id=1, replica_groups=mesh['req'=128,'tp'=4] {'req'}, dimensions={0} | all-to-all | bytes 917504 | tf_op jit(solution)/shard_map/all_to_all | solution.py:84
  371.1 2.0 reshape.89
  (36 shorter events, 6.2 us)
Async XLA Ops:
  6.5 43.5 %copy-start = (bf16[3,1408,352]{1,2,0:T(8,128)(2,1)S(1)}, bf16[3,1408,352]{1,2,0:T(8,128)(2,1)}, u32[]{:S(2)}) copy-start(bf16[3,1408,352]{1,2,0:T(8,128)(2,1)} %param.13) | copy-start | bytes 8921092
  6.5 43.5 %copy-start.5 = (f32[1408]{0:T(1024)S(1)}, f32[1408]{0:T(1024)}, u32[]{:S(2)}) copy-start(f32[1408]{0:T(1024)} %param.12) | copy-start | bytes 16900
  6.5 43.5 %copy-start.6 = (f32[1408]{0:T(1024)S(1)}, f32[1408]{0:T(1024)}, u32[]{:S(2)}) copy-start(f32[1408]{0:T(1024)} %param.11) | copy-start | bytes 16900
  6.5 40.0 %all-gather.5.cloned.1.call-start = ((), (), s32[]{:S(2)}) async-start(), calls=%async_computation.2 | async-start | bytes 1802240 | tf_op jit(solution)/shard_map/all_gather | solution.py:29
  7.3 87.8 %reduce-scatter.2.cloned.1.call-start = ((), (), s32[]{:S(2)}) async-start(), calls=%async_computation.3 | async-start | bytes 1802240 | tf_op jit(solution)/shard_map/reduce_scatter | solution.py:49
  46.5 3.6 copy-start.1
  57.8 2.8 copy-start.3
  60.6 34.5 %copy-start.2 = (bf16[512,352]{0,1:T(8,128)(2,1)S(1)}, bf16[512,352]{0,1:T(8,128)(2,1)}, u32[]{:S(2)}) copy-start(bf16[512,352]{0,1:T(8,128)(2,1)} %param.10) | copy-start | bytes 1081348
  62.7 54.8 %copy-start.4 = (s32[128,1]{0,1:T(1,128)S(1)}, s32[128,1]{0,1:T(1,128)}, u32[]{:S(2)}) copy-start(s32[128,1]{0,1:T(1,128)} %param.19) | copy-start | bytes 1540
  62.7 92.0 %all-gather.7.cloned.1.call-start = ((), (), s32[]{:S(2)}) async-start(), calls=%async_computation.4 | async-start | bytes 1802240 | tf_op jit(solution)/shard_map/all_gather | solution.py:63
  116.9 191.6 %all-gather.9.cloned.1.call-start = ((), (), s32[]{:S(2)}) async-start(), calls=%async_computation.5 | async-start | bytes 11096064 | tf_op jit(solution)/shard_map/all_gather | solution.py:67
Sparse Core Ops, SparseCore 0:
  9.4 37.0 all-gather.4
  62.8 32.1 reduce-scatter.1
  117.1 37.5 all-gather.6
  157.6 150.9 all-gather.8
where the time goes:
time: 381 us; the launch traced here: 380 us
  waiting for transfers between devices  257 us (67%)
  blocking collectives  54.5 us (14%)
  local copies, waits for them, and re-layouts  26.9 us (7%)
  matrix products  18.7 us (5%)
  between operations  13.3 us (3%)
  other arithmetic  9.11 us (2%)
    all_gather x1, waiting for transfers between devices, local(): lax.all_gather(merger_weight, 'req', axis=0, tiled=True)  151 us
    all_to_all x1, blocking collectives, local(): lax.all_to_all(outgoing, 'req', split_axis=0, concat_axis=0, tiled=True)  40.9 us
    all_gather x1, waiting for transfers between devices, local(): lax.all_gather(tokens, 'tp', axis=1, tiled=True).astype(jnp.float32)  37.2 us
    all_gather x1, waiting for transfers between devices, local(): full_groups = lax.all_gather(grouped, 'tp', axis=2, tiled=True)  36.7 us
    reduce_scatter x1, waiting for transfers between devices, local(): lax.psum_scatter(partial_value.astype(jnp.bfloat16), 'tp', scatter_dimens...  30.7 us
    unnamed x15, local copies, waits for them, and re-layouts  13.4 us
  transfers between devices with their start and end apart: 4, of which 4 were waited for; matrix products, arithmetic and copies ran while one was open for 2% of the time, Pallas kernels for 0%

commit v1 on v0

--- a/solution.py
+++ b/solution.py
@@ -60,7 +60,16 @@
     bias_part = lax.dynamic_slice_in_dim(ln2_bias, offset, col_width)
     patches = (shifted * lax.rsqrt(variance + epsilon) * gain_part + bias_part).astype(jnp.bfloat16)
     grouped = patches.reshape(group_count, 4, col_width)
-    full_groups = lax.all_gather(grouped, "tp", axis=2, tiled=True)
+    turn_the_sums_all = lambda local_x: jnp.concatenate(
+        lax.all_to_all(
+            jnp.stack([local_x for _ in range(lax.axis_size("tp"))]),
+            axis_name="tp",
+            split_axis=0,
+            concat_axis=0,
+        ),
+        2,
+    )
+    full_groups = turn_the_sums_all(grouped)
     merged = full_groups.reshape(group_count, 4 * full_width)
     projected = jnp.dot(
         merged,

time: 381 us -> 291 us (0.76)
  waiting for transfers between devices: 257 us -> 160 us
  starting transfers between devices: 0.12 us -> 4.42 us
    all_gather x1, waiting for transfers between devices: 151 us -> 78.2 us  [local(): lax.all_gather(merger_weight, 'req', axis=0, tiled=True)]
    all_gather x1 -> x0, waiting for transfers between devices: 36.7 us -> none  [local(): full_groups = lax.all_gather(grouped, 'tp', axis=2, tiled=True)]
    all_to_all x0 -> x1, waiting for transfers between devices: none -> 13.6 us  [local(): lax.all_to_all(jnp.stack([local_x for _ in range(lax.axis_size('tp'))]),...]
    all_to_all x0 -> x1, starting transfers between devices: none -> 4.33 us  [local(): lax.all_to_all(jnp.stack([local_x for _ in range(lax.axis_size('tp'))]),...]
  transfers between devices with their start and end apart: 4 -> 4, of which waited for: 4 -> 4; matrix products, arithmetic and copies ran while one was open for 2% -> 5% of each run, Pallas kernels for 0% -> 0%
where the time goes in v1:
time: 291 us; the launch traced here: 290 us
  waiting for transfers between devices  160 us (55%)
  blocking collectives  55.1 us (19%)
  local copies, waits for them, and re-layouts  27.3 us (9%)
  matrix products  18.6 us (6%)
  between operations  15 us (5%)
  other arithmetic  9.11 us (3%)
  starting transfers between devices  4.42 us (2%)
    all_gather x1, waiting for transfers between devices, local(): lax.all_gather(merger_weight, 'req', axis=0, tiled=True)  78.2 us
    all_to_all x1, blocking collectives, local(): lax.all_to_all(outgoing, 'req', split_axis=0, concat_axis=0, tiled=True)  41 us
    all_gather x1, waiting for transfers between devices, local(): lax.all_gather(tokens, 'tp', axis=1, tiled=True).astype(jnp.float32)  37.2 us
    reduce_scatter x1, waiting for transfers between devices, local(): lax.psum_scatter(partial_value.astype(jnp.bfloat16), 'tp', scatter_dimens...  30.2 us
    all_to_all x1, waiting for transfers between devices, local(): lax.all_to_all(jnp.stack([local_x for _ in range(lax.axis_size('tp'))]),...  13.6 us
    unnamed x15, local copies, waits for them, and re-layouts  13.4 us
    psum x1, blocking collectives, local(): row_total = lax.psum(jnp.sum(hidden, axis=1), 'tp')  7.81 us
    dot_general x1, matrix products, local(): jnp.dot(placing, projected, preferred_element_type=jnp.float32)  7.03 us
  transfers between devices with their start and end apart: 4, of which 4 were waited for; matrix products, arithmetic and copies ran while one was open for 5% of the time, Pallas kernels for 0%

profile of v1, /device:TPU:33, one launch (start us, length us, event | category | flops | bytes accessed | tf_op | source)
XLA Modules:
  0.0 290.0 jit_solution(3039078731299941668)
XLA Ops:
  10.1 37.2 %all-gather.4.cloned.1.call-done = bf16[512,1408]{0,1:T(8,128)(2,1)} async-done(((bf16[512,352]{0,1:T(8,128)(2,1)}), bf16[512,1408]{0,1:T(8,128)(2,1)}) %all-gather.4.cloned.1.call-update) | async-done | bytes 1441808 | tf_op jit(solution)/shard_map/all_gather | solution.py:29
  47.3 1.7 convert_reduce_fusion
  49.1 1.8 fusion.4
  50.9 2.0 fusion.18
  53.8 4.8 %fusion.31 = (f32[4,512]{1,0:T(4,128)S(1)}, f32[4,512,512]{1,2,0:T(8,128)}) fusion(pred[512,512]{0,1:T(8,128)(4,1)} %broadcast_compare_fusion, bf16[512,4,88]{0,2,1:T(8,128)(2,1)} %bitcast.33, bf16[512,4,88]{0,2,1:T(8,128)(2,1)} %bitcast.32), kind=kOutput, calls=%fused_computation.48 | convolution fusion | flops 188744192 | bytes 5185536 | tf_op jit(solution)/shard_map/sub | solution.py:44
  58.6 2.8 fusion.21
  61.4 2.1 convolution_convert_fusion
  65.6 30.2 %reduce-scatter.2.cloned.1.call-done = bf16[512,352]{0,1:T(8,128)(2,1)} async-done(((bf16[512,1408]{0,1:T(8,128)(2,1)}), bf16[512,352]{0,1:T(8,128)(2,1)}) %reduce-scatter.2.cloned.1.call-update) | async-done | bytes 360464 | tf_op jit(solution)/shard_map/reduce_scatter | solution.py:49
  97.0 7.8 %psum.14 = f32[512]{0:T(512)S(1)} all-reduce(f32[512]{0:T(512)S(1)} %fusion.23), channel_id=1, replica_groups=mesh['req'=128,'tp'=4] {'tp'}, use_global_device_ids=true, to_apply=%region_8.9 | all-reduce | flops 512 | bytes 4096 | tf_op jit(solution)/shard_map/psum | solution.py:53
  104.8 1.1 multiply_reduce_fusion
  105.9 6.3 %psum.15 = f32[512]{0:T(512)S(1)} all-reduce(f32[512]{0:T(512)S(1)} %multiply_reduce_fusion), channel_id=1, replica_groups=mesh['req'=128,'tp'=4] {'tp'}, use_global_device_ids=true, to_apply=%region_10.11 | all-reduce | flops 512 | bytes 4096 | tf_op jit(solution)/shard_map/psum | solution.py:56
  112.2 1.9 add_convert_fusion
  114.2 1.2 copy.20
  116.2 1.3 copy.21
  117.5 1.4 stack.3
  118.9 4.3 %all-to-all-start = ((bf16[4,128,4,352]{1,3,2,0:T(8,128)(2,1)}), bf16[4,128,4,352]{1,3,2,0:T(8,128)(2,1)}, u32[]{:S(2)}, u32[]{:S(2)}) async-start(bf16[4,128,4,352]{1,3,2,0:T(8,128)(2,1)} %stack.3), calls=%async_computation.1 | async-start | bytes 2883584 | tf_op jit(solution)/shard_map/all_to_all | solution.py:64
  123.7 13.6 %all-to-all-done = bf16[4,128,4,352]{1,3,2,0:T(8,128)(2,1)} async-done(((bf16[4,128,4,352]{1,3,2,0:T(8,128)(2,1)}), bf16[4,128,4,352]{1,3,2,0:T(8,128)(2,1)}, u32[]{:S(2)}, u32[]{:S(2)}) %all-to-all-start) | async-done | bytes 1441824 | tf_op jit(solution)/shard_map/all_to_all | solution.py:64
  137.2 2.6 copy.22
  139.8 78.2 %all-gather.6.cloned.1.call-done = bf16[128,44,896]{2,1,0:T(8,128)(2,1)} async-done(((bf16[1,44,896]{2,1,0:T(8,128)(2,1)}), bf16[128,44,896]{2,1,0:T(8,128)(2,1)}) %all-gather.6.cloned.1.call-update) | async-done | bytes 10092560 | tf_op jit(solution)/shard_map/all_gather | solution.py:76
  218.0 13.4 %reshape.89 = bf16[5632,896]{1,0:T(8,128)(2,1)} reshape(bf16[128,44,896]{2,1,0:T(8,128)(2,1)} %all-gather.6.cloned.1.call-done) | data formatting | bytes 20185088
  231.4 7.0 %convolution_convert_fusion.2 = bf16[256,896]{1,0:T(8,128)(2,1)} fusion(bf16[128,5632]{0,1:T(8,128)(2,1)} %bitcast.30, bf16[5632,896]{1,0:T(8,128)(2,1)} %reshape.89, s32[128]{0:T(128)S(1)} %multiply_add_fusion), kind=kOutput, calls=%fused_computation.25 | convolution fusion | flops 1350942720 | bytes 11993600 | tf_op jit(solution)/shard_map/dot_general | solution.py:91
  238.5 1.2 reshape.86
  239.6 41.0 %all_to_all.10 = bf16[128,2,896]{2,1,0:T(2,128)(2,1)} all-to-all(bf16[128,2,896]{2,1,0:T(2,128)(2,1)S(1)} %reshape.86), channel_id=1, replica_groups=mesh['req'=128,'tp'=4] {'req'}, dimensions={0} | all-to-all | bytes 917504 | tf_op jit(solution)/shard_map/all_to_all | solution.py:93
  280.6 2.0 reshape.87
  (36 shorter events, 8.2 us)
Async XLA Ops:
  7.4 43.5 %copy-start = (bf16[3,1408,352]{1,2,0:T(8,128)(2,1)S(1)}, bf16[3,1408,352]{1,2,0:T(8,128)(2,1)}, u32[]{:S(2)}) copy-start(bf16[3,1408,352]{1,2,0:T(8,128)(2,1)} %param.13) | copy-start | bytes 8921092
  7.4 43.5 %copy-start.5 = (f32[1408]{0:T(1024)S(1)}, f32[1408]{0:T(1024)}, u32[]{:S(2)}) copy-start(f32[1408]{0:T(1024)} %param.12) | copy-start | bytes 16900
  7.4 43.5 %copy-start.6 = (f32[1408]{0:T(1024)S(1)}, f32[1408]{0:T(1024)}, u32[]{:S(2)}) copy-start(f32[1408]{0:T(1024)} %param.11) | copy-start | bytes 16900
  7.4 40.0 %all-gather.4.cloned.1.call-start = ((), (), s32[]{:S(2)}) async-start(), calls=%async_computation.3 | async-start | bytes 1802240 | tf_op jit(solution)/shard_map/all_gather | solution.py:29
  8.1 87.8 %reduce-scatter.2.cloned.1.call-start = ((), (), s32[]{:S(2)}) async-start(), calls=%async_computation.4 | async-start | bytes 1802240 | tf_op jit(solution)/shard_map/reduce_scatter | solution.py:49
  47.3 3.6 %copy-start.1 = (bf16[512,1408]{0,1:T(8,128)(2,1)S(1)}, bf16[512,1408]{0,1:T(8,128)(2,1)}, u32[]{:S(2)}) copy-start(bf16[512,1408]{0,1:T(8,128)(2,1)} %all-gather.4.cloned.1.call-done) | copy-start | bytes 4325380
  58.6 2.8 copy-start.3
  61.4 34.4 %copy-start.2 = (bf16[512,352]{0,1:T(8,128)(2,1)S(1)}, bf16[512,352]{0,1:T(8,128)(2,1)}, u32[]{:S(2)}) copy-start(bf16[512,352]{0,1:T(8,128)(2,1)} %param.10) | copy-start | bytes 1081348
  63.5 154.5 %all-gather.6.cloned.1.call-start = ((), (), s32[]{:S(2)}) async-start(), calls=%async_computation.5 | async-start | bytes 11096064 | tf_op jit(solution)/shard_map/all_gather | solution.py:76
  116.2 7.0 %copy-start.4 = (s32[128,1]{0,1:T(1,128)S(1)}, s32[128,1]{0,1:T(1,128)}, u32[]{:S(2)}) copy-start(s32[128,1]{0,1:T(1,128)} %param.19) | copy-start | bytes 1540
  118.9 18.4 %all-to-all-start = ((bf16[4,128,4,352]{1,3,2,0:T(8,128)(2,1)}), bf16[4,128,4,352]{1,3,2,0:T(8,128)(2,1)}, u32[]{:S(2)}, u32[]{:S(2)}) async-start(bf16[4,128,4,352]{1,3,2,0:T(8,128)(2,1)} %stack.3), calls=%async_computation.1 | async-start | bytes 2883584 | tf_op jit(solution)/shard_map/all_to_all | solution.py:64
Sparse Core Ops, SparseCore 0:
  10.3 37.0 all-gather.3
  63.6 32.1 reduce-scatter.1
Sparse Core Ops, SparseCore 1:
  67.0 150.9 all-gather.5
